TPU v7x, 32 devices: a whole 2x2x4 slice. The times are simulated.
32 devices in a mesh: row: 4 (over y, x), col: 8 (over z, core).
Axes of the slice: x: 2, y: 2, z: 4, core: 2. Of those that a mesh axis runs over, the one named last changes fastest.
Arguments:
- teacher: bfloat16 [16384, 256], replicated, may hold values from -4 to 4
- panel_ids: int32 [2048], P('col'), may hold values from 0 to 16383
- rest_ids: int32 [4, 8, 128], P('row', 'col'), may hold values from 0 to 16383
- inverse: bfloat16 [2048, 2048], replicated, may hold values from -1 to 1, as said below
Outputs:
- trailing: float32 [8, 4, 128, 4, 8, 128], P(None, 'row', None, None, 'col')
- panel_rows: bfloat16 [4, 8, 128, 2048], P('row', 'col')
Inputs may be any that keep to these rules, and one draw needn't show every extreme that they name: `inverse`: zero above the diagonal.
All inputs are finite; a program needn't handle non-finite values.
Results may differ from a plain program's by a relative error of at most 0.0049.
Values may be sent and summed in bfloat16 or wider, within the bound.
A program may use at most 128 MiB of HBM per device.

v0:
```python
import jax
import jax.numpy as jnp
from jax import lax
from jax.sharding import PartitionSpec as P


def gaussian(left_rows, right_rows, inv_scale):
    sq_left = jnp.sum(jnp.square(left_rows.astype(jnp.float32)), axis=-1)
    sq_right = jnp.sum(jnp.square(right_rows.astype(jnp.float32)), axis=-1)
    inner = lax.dot_general(
        left_rows, right_rows, (((1,), (1,)), ((), ())), preferred_element_type=jnp.float32
    )
    return jnp.exp(-inv_scale * (sq_left[:, None] + sq_right[None, :] - 2.0 * inner))


def factor(rows_emb, panel_emb, inverse, inv_scale):
    kernel = gaussian(rows_emb, panel_emb, inv_scale).astype(jnp.bfloat16)
    block_width = inverse.shape[0] // 4
    pieces = []
    for block_at in range(4):
        finish = (block_at + 1) * block_width
        pieces.append(
            lax.dot_general(
                kernel[:, :finish],
                inverse[block_at * block_width : finish, :finish],
                (((1,), (1,)), ((), ())),
                preferred_element_type=jnp.float32,
            )
        )
    return jnp.concatenate(pieces, 1).astype(jnp.bfloat16)


def shards(teacher, panel_ids, rest_ids, inverse):
    n_row = lax.axis_size("row")
    n_col = lax.axis_size("col")
    row_at = lax.axis_index("row")
    col_at = lax.axis_index("col")
    stretch_rows = rest_ids.shape[2]
    inv_scale = 2.0 / teacher.shape[1]
    gathered = lax.all_gather(rest_ids, ("row", "col"), axis=0, tiled=True)
    blocks = gathered.reshape(n_row * n_col, stretch_rows)
    panel = lax.all_gather(panel_ids, "col", axis=0, tiled=True)
    panel_emb = teacher[panel]
    own_ids = lax.dynamic_slice_in_dim(blocks, row_at * n_col + col_at, 1, 0).reshape(stretch_rows)
    col_ids = lax.dynamic_slice_in_dim(
        blocks.reshape(n_row, n_col, stretch_rows), col_at, 1, 1
    ).reshape(-1)
    row_ids = lax.dynamic_slice_in_dim(
        blocks.reshape(n_col, n_row, stretch_rows), row_at, 1, 1
    ).reshape(-1)
    own_factor = factor(teacher[own_ids], panel_emb, inverse, inv_scale)
    col_emb = teacher[col_ids]
    col_factor = lax.all_gather(own_factor, "row", axis=0, tiled=True)
    row_emb = teacher[row_ids]
    kernel = gaussian(row_emb, col_emb, inv_scale)
    row_factor = factor(row_emb, panel_emb, inverse, inv_scale)
    update = lax.dot_general(
        row_factor, col_factor, (((1,), (1,)), ((), ())), preferred_element_type=jnp.float32
    )
    rows_local = jnp.arange(n_col * stretch_rows, dtype=jnp.int32)
    row_index = (
        rows_local // stretch_rows * n_row + row_at
    ) * stretch_rows + rows_local % stretch_rows
    cols_local = jnp.arange(n_row * stretch_rows, dtype=jnp.int32)
    col_index = (
        cols_local // stretch_rows * n_col + col_at
    ) * stretch_rows + cols_local % stretch_rows
    result = kernel - update
    trailing = jnp.where(row_index[:, None] >= col_index[None, :], result, jnp.zeros_like(result))
    return (
        trailing.reshape(n_col, 1, stretch_rows, n_row, 1, stretch_rows),
        own_factor.reshape(1, 1, stretch_rows, own_factor.shape[1]),
    )


def solution(mesh):
    return jax.shard_map(
        shards,
        mesh=mesh,
        in_specs=(P(), P("col"), P("row", "col", None), P()),
        out_specs=(P(None, "row", None, None, "col", None), P("row", "col", None, None)),
        check_vma=False,
    )
```

profile of v0, /device:TPU:0, one launch (start us, length us, event | category | flops | bytes accessed | tf_op | source)
XLA Modules:
  0.0 132.2 jit_solution(9935352924947401463)
XLA Ops:
  7.2 0.0 all-gather.3.cloned.1.call-start
  7.2 43.5 %all_gather.9 = s32[32,1,128]{2,1,0:T(1,128)S(1)} all-gather(s32[1,1,128]{2,1,0:T(1,128)} %param.6), channel_id=1, replica_groups=mesh['row'=4,'col'=8] {'row','col'}, dimensions={0}, use_global_device_ids=true | all-gather | bytes 16896 | tf_op jit(solution)/shard_map/all_gather | solution.py:40
  50.7 5.2 %gather_fusion.3 = bf16[128,256]{1,0:T(8,128)(2,1)S(1)} fusion(bf16[16384,256]{1,0:T(8,128)(2,1)} %param.4, s32[1024]{0:T(1024)S(1)} %pad_clamp_fusion), kind=kCustom, calls=%fused_computation.3 | custom fusion | bytes 131584 | tf_op jit(solution)/shard_map/gather | solution.py:51
  55.9 0.1 multiply_reduce_fusion.3
  56.0 9.0 %all-gather = s32[8,1,256]{2,1,0:T(1,128)S(1)} all-gather(s32[1,1,256]{2,1,0:T(1,128)} %bitcast.42), channel_id=1, replica_groups=mesh['row'=4,'col'=8] {'col'}, dimensions={0}, use_global_device_ids=true | all-gather | bytes 9216 | tf_op jit(solution)/shard_map/all_gather | solution.py:42
  65.0 11.1 %gather_fusion.2 = bf16[2048,256]{1,0:T(8,128)(2,1)S(1)} fusion(bf16[16384,256]{1,0:T(8,128)(2,1)} %param.4, s32[2048]{0:T(1024)S(1)} %fusion.46), kind=kCustom, calls=%fused_computation.2 | custom fusion | bytes 2105344 | tf_op jit(solution)/shard_map/gather | solution.py:43
  76.1 0.3 multiply_reduce_fusion
  76.5 0.5 fusion.13
  77.0 1.3 %convolution_convert_fusion.1 = bf16[128,512]{1,0:T(8,128)(2,1)S(1)} fusion(bf16[2048,2048]{1,0:T(8,128)(2,1)} %param.7, bf16[128,2048]{1,0:T(8,128)(2,1)S(1)} %fusion.13), kind=kOutput, calls=%fused_computation.36 | convolution fusion | flops 67174400 | bytes 786432 | tf_op jit(solution)/shard_map/dot_general | solution.py:23
  78.4 1.7 %convolution_convert_fusion.2 = bf16[128,512]{1,0:T(8,128)(2,1)S(1)} fusion(bf16[2048,2048]{1,0:T(8,128)(2,1)} %param.7, bf16[128,2048]{1,0:T(8,128)(2,1)S(1)} %fusion.13), kind=kOutput, calls=%fused_computation.37 | convolution fusion | flops 134283264 | bytes 1441792 | tf_op jit(solution)/shard_map/dot_general | solution.py:23
  80.1 2.4 %fusion.32 = bf16[128,512]{1,0:T(8,128)(2,1)S(1)} fusion(bf16[128,2048]{1,0:T(8,128)(2,1)S(1)} %fusion.13, bf16[2048,2048]{1,0:T(8,128)(2,1)} %param.7), kind=kOutput, calls=%fused_computation.35 | convolution fusion | flops 268500992 | bytes 2752512 | tf_op jit(solution)/shard_map/dot_general | solution.py:23
  82.5 2.1 %fusion.35 = bf16[128,512]{1,0:T(8,128)(2,1)S(1)} fusion(bf16[2048,2048]{1,0:T(8,128)(2,1)} %param.7, bf16[128,2048]{1,0:T(8,128)(2,1)S(1)} %fusion.13), kind=kOutput, calls=%fused_computation.38 | convolution fusion | flops 201392128 | bytes 2097152 | tf_op jit(solution)/shard_map/dot_general | solution.py:23
  84.6 0.8 pad_maximum_fusion
  85.4 0.0 all-gather.3.cloned.1.call-update
  85.5 7.9 %gather_fusion = bf16[1024,256]{1,0:T(8,128)(2,1)S(1)} fusion(bf16[16384,256]{1,0:T(8,128)(2,1)} %param.4, s32[1024]{0:T(1024)S(1)} %broadcast_clamp_fusion), kind=kCustom, calls=%fused_computation | custom fusion | bytes 1052672 | tf_op jit(solution)/shard_map/gather | solution.py:54
  93.4 6.0 %gather_fusion.1 = bf16[512,256]{1,0:T(8,128)(2,1)S(1)} fusion(bf16[16384,256]{1,0:T(8,128)(2,1)} %param.4, s32[1024]{0:T(1024)S(1)} %pad_clamp_fusion.1), kind=kCustom, calls=%fused_computation.1 | custom fusion | bytes 526336 | tf_op jit(solution)/shard_map/gather | solution.py:52
  99.5 0.1 multiply_reduce_fusion.2
  99.7 0.2 multiply_reduce_fusion.1
  99.9 0.0 slice-start
  99.9 0.8 pad_maximum_fusion.1
  100.7 0.0 slice-start.1
  100.7 2.6 %exponential_convert_fusion = bf16[1024,2048]{1,0:T(8,128)(2,1)S(1)} fusion(bf16[1024,256]{1,0:T(8,128)(2,1)S(1)} %gather_fusion, bf16[2048,256]{1,0:T(8,128)(2,1)S(1)} %gather_fusion.2, f32[2048]{0:T(1024)S(1)} %multiply_reduce_fusion, f32[1024]{0:T(1024)S(1)} %multiply_reduce_fusion.1), kind=kOutput, calls=%fused_computation.4 | convolution fusion | flops 1084227584 | bytes 5779456 | tf_op jit(solution)/shard_map/dot_general | solution.py:10
  103.3 0.0 slice-done
  103.3 0.4 slice-done.1
  103.7 0.7 convolution_convert_fusion
  104.4 1.3 fusion.20
  105.7 2.8 %fusion.23 = bf16[1024,512]{1,0:T(8,128)(2,1)} fusion(bf16[1024,2048]{1,0:T(8,128)(2,1)S(1)} %exponential_convert_fusion, bf16[2048,2048]{1,0:T(8,128)(2,1)S(1)} %bitcast.44), kind=kOutput, calls=%fused_computation.29 | convolution fusion | flops 1611137024 | bytes 5767168 | tf_op jit(solution)/shard_map/dot_general | solution.py:23
  108.5 3.3 %fusion.26 = bf16[1024,512]{1,0:T(8,128)(2,1)} fusion(bf16[1024,2048]{1,0:T(8,128)(2,1)S(1)} %exponential_convert_fusion, bf16[2048,2048]{1,0:T(8,128)(2,1)S(1)} %bitcast.44), kind=kOutput, calls=%fused_computation.31 | convolution fusion | flops 2148007936 | bytes 7340032 | tf_op jit(solution)/shard_map/dot_general | solution.py:23
  111.9 6.3 %all-gather.3.cloned.1.call-done = bf16[512,2048]{1,0:T(8,128)(2,1)} async-done(((bf16[128,2048]{1,0:T(8,128)(2,1)}), bf16[512,2048]{1,0:T(8,128)(2,1)}) %all-gather.3.cloned.1.call-update) | async-done | bytes 2097168 | tf_op jit(solution)/shard_map/all_gather | solution.py:53
  118.2 4.5 %fusion = f32[1024,512]{1,0:T(8,128)S(1)} fusion(bf16[512,2048]{1,0:T(8,128)(2,1)} %all-gather.3.cloned.1.call-done, bf16[1024,512]{1,0:T(8,128)(2,1)} %fusion.26, bf16[1024,512]{1,0:T(8,128)(2,1)} %fusion.23, bf16[1024,512]{1,0:T(8,128)(2,1)S(1)} %fusion.20, bf16[1024,512]{1,0:T(8,128)(2,1)S(1)} %convolution_convert_fusion), kind=kOutput, calls=%fused_computation.5 | convolution fusion | flops 2164260864 | bytes 8388608 | tf_op jit(solution)/shard_map/dot_general | solution.py:57
  122.8 0.8 subtract_select_fusion
  123.6 1.7 %reshape.218 = f32[8,1,128,4,1,128]{5,3,2,0,4,1:T(4,128)} reshape(f32[1024,512]{1,0:T(8,128)S(1)} %subtract_select_fusion) | data formatting | bytes 4194304 | tf_op jit(solution)/shard_map/reshape | solution.py:71
  (10 shorter events, 0.1 us)
Async XLA Ops:
  7.2 111.1 %all-gather.3.cloned.1.call-start = ((), (), s32[]{:S(2)}) async-start(), calls=%async_computation | async-start | bytes 2621440 | tf_op jit(solution)/shard_map/all_gather | solution.py:53
  99.9 3.4 %slice-start = ((s8[8388608]{0:T(1024)(128)(4,1)}), s8[4194304]{0:T(1024)(128)(4,1)S(1)}, s32[]{:S(2)}) async-start(s8[8388608]{0:T(1024)(128)(4,1)} %bitcast.43), calls=%async_computation.1 | async-start | bytes 8388608
  100.7 3.0 %slice-start.1 = ((s8[8388608]{0:T(1024)(128)(4,1)}), s8[4194304]{0:T(1024)(128)(4,1)S(1)}, s32[]{:S(2)}) async-start(s8[8388608]{0:T(1024)(128)(4,1)} %bitcast.43), calls=%async_computation.2 | async-start | bytes 8388608
Sparse Core Ops, SparseCore 0:
  85.6 32.6 all-gather.2
where the time goes:
time: 133 us; the launch traced here: 132 us
  blocking collectives  52.5 us (39%)
  local copies, waits for them, and re-layouts  32.4 us (24%)
  matrix products  24.1 us (18%)
  between operations  14.2 us (11%)
  waiting for transfers between devices  6.36 us (5%)
  other arithmetic  2.57 us (2%)
    all_gather x1, blocking collectives, shards(): gathered = lax.all_gather(rest_ids, ('row', 'col'), axis=0, tiled=True)  43.5 us
    dot_general x8, matrix products, factor(): lax.dot_general(kernel[:, :finish], inverse[block_at * block_width:finish...  15.7 us
    gather x1, local copies, waits for them, and re-layouts, shards(): panel_emb = teacher[panel]  11.1 us
    all_gather x1, blocking collectives, shards(): panel = lax.all_gather(panel_ids, 'col', axis=0, tiled=True)  8.99 us
    gather x1, local copies, waits for them, and re-layouts, shards(): row_emb = teacher[row_ids]  7.92 us
    all_gather x1, waiting for transfers between devices, shards(): col_factor = lax.all_gather(own_factor, 'row', axis=0, tiled=True)  6.34 us
    gather x1, local copies, waits for them, and re-layouts, shards(): col_emb = teacher[col_ids]  6.02 us
    gather x1, local copies, waits for them, and re-layouts, shards(): own_factor = factor(teacher[own_ids], panel_emb, inverse, inv_scale)  5.22 us
  transfers between devices with their start and end apart: 1, of which 1 were waited for; matrix products, arithmetic and copies ran while one was open for 20% of the time, Pallas kernels for 0%

commit v1 on v0

--- a/solution.py
+++ b/solution.py
@@ -2,6 +2,12 @@
 import jax.numpy as jnp
 from jax import lax
 from jax.sharding import PartitionSpec as P
+
+
+def in_order(blocks, dim):
+    blocks = jnp.moveaxis(blocks, 0, dim)
+    dims = blocks.shape
+    return blocks.reshape(*dims[:dim], dims[dim] * dims[dim + 1], *dims[dim + 2 :])
 
 
 def gaussian(left_rows, right_rows, inv_scale):
@@ -39,7 +45,14 @@
     inv_scale = 2.0 / teacher.shape[1]
     gathered = lax.all_gather(rest_ids, ("row", "col"), axis=0, tiled=True)
     blocks = gathered.reshape(n_row * n_col, stretch_rows)
-    panel = lax.all_gather(panel_ids, "col", axis=0, tiled=True)
+    size = lax.axis_size("col")
+    upward = [(i, (i + 1) % size) for i in range(size)]
+    blocks_2 = [panel_ids]
+    while len(blocks_2) < size:
+        blocks_2.append(lax.ppermute(blocks_2[-1], "col", upward))
+    position = lax.axis_index("col")
+    blocks_2 = jnp.stack(blocks_2)[(position - jnp.arange(size)) % size]
+    panel = in_order(blocks_2, 0)
     panel_emb = teacher[panel]
     own_ids = lax.dynamic_slice_in_dim(blocks, row_at * n_col + col_at, 1, 0).reshape(stretch_rows)
     col_ids = lax.dynamic_slice_in_dim(

time: 133 us -> 153 us (1.15)
  waiting for transfers between devices: 6.36 us -> 34.8 us
  blocking collectives: 52.5 us -> 43 us
    ppermute x0 -> x7, waiting for transfers between devices: none -> 18.7 us  [shards(): blocks_2.append(lax.ppermute(blocks_2[-1], 'col', upward))]
    all_gather x1, waiting for transfers between devices: 6.34 us -> 16.1 us  [shards(): col_factor = lax.all_gather(own_factor, 'row', axis=0, tiled=True)]
    all_gather x1 -> x0, blocking collectives: 8.99 us -> none  [shards(): panel = lax.all_gather(panel_ids, 'col', axis=0, tiled=True)]
  transfers between devices with their start and end apart: 1 -> 8, of which waited for: 1 -> 5; matrix products, arithmetic and copies ran while one was open for 20% -> 20% of each run, Pallas kernels for 0% -> 0%
where the time goes in v1:
time: 153 us
  blocking collectives  43 us (28%)
  waiting for transfers between devices  34.8 us (23%)
  local copies, waits for them, and re-layouts  33.2 us (22%)
  matrix products  24.1 us (16%)
  between operations  14.3 us (9%)
  other arithmetic  2.59 us (2%)
    all_gather x1, blocking collectives, shards(): gathered = lax.all_gather(rest_ids, ('row', 'col'), axis=0, tiled=True)  43 us
    ppermute x7, waiting for transfers between devices, shards(): blocks_2.append(lax.ppermute(blocks_2[-1], 'col', upward))  18.7 us
    all_gather x1, waiting for transfers between devices, shards(): col_factor = lax.all_gather(own_factor, 'row', axis=0, tiled=True)  16.1 us
    dot_general x8, matrix products, factor(): lax.dot_general(kernel[:, :finish], inverse[block_at * block_width:finish...  15.7 us
    gather x1, local copies, waits for them, and re-layouts, shards(): panel_emb = teacher[panel]  11.1 us
    gather x1, local copies, waits for them, and re-layouts, shards(): row_emb = teacher[row_ids]  7.92 us
    gather x1, local copies, waits for them, and re-layouts, shards(): col_emb = teacher[col_ids]  6.02 us
    gather x1, local copies, waits for them, and re-layouts, shards(): own_factor = factor(teacher[own_ids], panel_emb, inverse, inv_scale)  5.22 us
  transfers between devices with their start and end apart: 8, of which 5 were waited for; matrix products, arithmetic and copies ran while one was open for 20% of the time, Pallas kernels for 0%

profile of v1, /device:TPU:0, one launch (start us, length us, event | category | flops | bytes accessed | tf_op | source)
XLA Modules:
  0.0 153.0 jit_solution(10835155268741538277)
XLA Ops:
  7.2 0.5 collective-permute-start
  7.8 43.0 %all_gather.6 = s32[32,1,128]{2,1,0:T(1,128)S(1)} all-gather(s32[1,1,128]{2,1,0:T(1,128)} %param.6), channel_id=1, replica_groups=mesh['row'=4,'col'=8] {'row','col'}, dimensions={0}, use_global_device_ids=true | all-gather | bytes 16896 | tf_op jit(solution)/shard_map/all_gather | solution.py:46
  50.8 0.4 collective-permute-start.1
  51.2 4.5 %collective-permute-done.1 = s32[256]{0:T(256)S(1)} collective-permute-done((s32[256]{0:T(256)S(1)}, s32[256]{0:T(256)S(1)}, u32[]{:S(2)}, u32[]{:S(2)}) %collective-permute-start.1) | collective-permute-done | bytes 1056 | tf_op jit(solution)/shard_map/ppermute | solution.py:52
  55.7 5.2 %gather_fusion.4 = bf16[128,256]{1,0:T(8,128)(2,1)S(1)} fusion(bf16[16384,256]{1,0:T(8,128)(2,1)} %param.4, s32[1024]{0:T(1024)S(1)} %pad_clamp_fusion), kind=kCustom, calls=%fused_computation.4 | custom fusion | bytes 131584 | tf_op jit(solution)/shard_map/gather | solution.py:64
  61.1 4.7 %collective-permute-done.3 = s32[256]{0:T(256)S(1)} collective-permute-done((s32[256]{0:T(256)S(1)}, s32[256]{0:T(256)S(1)}, u32[]{:S(2)}, u32[]{:S(2)}) %collective-permute-start.3) | collective-permute-done | bytes 1056 | tf_op jit(solution)/shard_map/ppermute | solution.py:52
  65.8 4.8 %collective-permute-done.4 = s32[256]{0:T(256)S(1)} collective-permute-done((s32[256]{0:T(256)S(1)}, s32[256]{0:T(256)S(1)}, u32[]{:S(2)}, u32[]{:S(2)}) %collective-permute-start.4) | collective-permute-done | bytes 1056 | tf_op jit(solution)/shard_map/ppermute | solution.py:52
  70.6 4.8 %collective-permute-done.5 = s32[256]{0:T(256)S(1)} collective-permute-done((s32[256]{0:T(256)S(1)}, s32[256]{0:T(256)S(1)}, u32[]{:S(2)}, u32[]{:S(2)}) %collective-permute-start.5) | collective-permute-done | bytes 1056 | tf_op jit(solution)/shard_map/ppermute | solution.py:52
  75.4 7.9 %gather_fusion = bf16[1024,256]{1,0:T(8,128)(2,1)S(1)} fusion(bf16[16384,256]{1,0:T(8,128)(2,1)} %param.4, s32[1024]{0:T(1024)S(1)} %broadcast_clamp_fusion.1), kind=kCustom, calls=%fused_computation | custom fusion | bytes 1052672 | tf_op jit(solution)/shard_map/gather | solution.py:67
  83.4 0.6 gather_fusion.2
  84.0 11.1 %gather_fusion.3 = bf16[2048,256]{1,0:T(8,128)(2,1)S(1)} fusion(bf16[16384,256]{1,0:T(8,128)(2,1)} %param.4, s32[2048]{0:T(1024)S(1)} %broadcast_clamp_fusion), kind=kCustom, calls=%fused_computation.3 | custom fusion | bytes 2105344 | tf_op jit(solution)/shard_map/gather | solution.py:56
  95.1 0.3 multiply_reduce_fusion
  95.4 0.5 fusion.13
  95.9 1.3 convolution_convert_fusion.1
  97.3 1.7 %convolution_convert_fusion.2 = bf16[128,512]{1,0:T(8,128)(2,1)S(1)} fusion(bf16[2048,2048]{1,0:T(8,128)(2,1)} %param.7, bf16[128,2048]{1,0:T(8,128)(2,1)S(1)} %fusion.13), kind=kOutput, calls=%fused_computation.38 | convolution fusion | flops 134283264 | bytes 1441792 | tf_op jit(solution)/shard_map/dot_general | solution.py:29
  99.0 2.4 %fusion.32 = bf16[128,512]{1,0:T(8,128)(2,1)S(1)} fusion(bf16[128,2048]{1,0:T(8,128)(2,1)S(1)} %fusion.13, bf16[2048,2048]{1,0:T(8,128)(2,1)} %param.7), kind=kOutput, calls=%fused_computation.36 | convolution fusion | flops 268500992 | bytes 2752512 | tf_op jit(solution)/shard_map/dot_general | solution.py:29
  101.4 2.1 %fusion.35 = bf16[128,512]{1,0:T(8,128)(2,1)S(1)} fusion(bf16[2048,2048]{1,0:T(8,128)(2,1)} %param.7, bf16[128,2048]{1,0:T(8,128)(2,1)S(1)} %fusion.13), kind=kOutput, calls=%fused_computation.39 | convolution fusion | flops 201392128 | bytes 2097152 | tf_op jit(solution)/shard_map/dot_general | solution.py:29
  103.5 0.8 pad_maximum_fusion
  104.4 6.0 %gather_fusion.1 = bf16[512,256]{1,0:T(8,128)(2,1)S(1)} fusion(bf16[16384,256]{1,0:T(8,128)(2,1)} %param.4, s32[1024]{0:T(1024)S(1)} %pad_clamp_fusion.2), kind=kCustom, calls=%fused_computation.1 | custom fusion | bytes 526336 | tf_op jit(solution)/shard_map/gather | solution.py:65
  110.4 0.1 multiply_reduce_fusion.2
  110.6 0.2 multiply_reduce_fusion.1
  110.8 0.8 pad_maximum_fusion.1
  111.7 2.6 %exponential_convert_fusion = bf16[1024,2048]{1,0:T(8,128)(2,1)S(1)} fusion(bf16[1024,256]{1,0:T(8,128)(2,1)S(1)} %gather_fusion, bf16[2048,256]{1,0:T(8,128)(2,1)S(1)} %gather_fusion.3, f32[2048]{0:T(1024)S(1)} %multiply_reduce_fusion, f32[1024]{0:T(1024)S(1)} %multiply_reduce_fusion.1), kind=kOutput, calls=%fused_computation.5 | convolution fusion | flops 1084227584 | bytes 5779456 | tf_op jit(solution)/shard_map/dot_general | solution.py:16
  114.3 0.6 slice-done.1
  114.8 0.7 convolution_convert_fusion
  115.6 1.3 fusion.20
  116.8 2.8 %fusion.23 = bf16[1024,512]{1,0:T(8,128)(2,1)} fusion(bf16[1024,2048]{1,0:T(8,128)(2,1)S(1)} %exponential_convert_fusion, bf16[2048,2048]{1,0:T(8,128)(2,1)S(1)} %bitcast.66), kind=kOutput, calls=%fused_computation.30 | convolution fusion | flops 1611137024 | bytes 5767168 | tf_op jit(solution)/shard_map/dot_general | solution.py:29
  119.7 3.3 %fusion.26 = bf16[1024,512]{1,0:T(8,128)(2,1)} fusion(bf16[1024,2048]{1,0:T(8,128)(2,1)S(1)} %exponential_convert_fusion, bf16[2048,2048]{1,0:T(8,128)(2,1)S(1)} %bitcast.66), kind=kOutput, calls=%fused_computation.32 | convolution fusion | flops 2148007936 | bytes 7340032 | tf_op jit(solution)/shard_map/dot_general | solution.py:29
  123.0 16.1 %all-gather.2.cloned.1.call-done = bf16[512,2048]{1,0:T(8,128)(2,1)} async-done(((bf16[128,2048]{1,0:T(8,128)(2,1)}), bf16[512,2048]{1,0:T(8,128)(2,1)}) %all-gather.2.cloned.1.call-update) | async-done | bytes 2097168 | tf_op jit(solution)/shard_map/all_gather | solution.py:66
  139.0 4.5 %fusion = f32[1024,512]{1,0:T(8,128)S(1)} fusion(bf16[512,2048]{1,0:T(8,128)(2,1)} %all-gather.2.cloned.1.call-done, bf16[1024,512]{1,0:T(8,128)(2,1)} %fusion.26, bf16[1024,512]{1,0:T(8,128)(2,1)} %fusion.23, bf16[1024,512]{1,0:T(8,128)(2,1)S(1)} %fusion.20, bf16[1024,512]{1,0:T(8,128)(2,1)S(1)} %convolution_convert_fusion), kind=kOutput, calls=%fused_computation.6 | convolution fusion | flops 2164260864 | bytes 8388608 | tf_op jit(solution)/shard_map/dot_general | solution.py:70
  143.6 0.8 subtract_select_fusion
  144.4 1.7 %reshape.299 = f32[8,1,128,4,1,128]{5,3,2,0,4,1:T(4,128)} reshape(f32[1024,512]{1,0:T(8,128)S(1)} %subtract_select_fusion) | data formatting | bytes 4194304 | tf_op jit(solution)/shard_map/reshape | solution.py:84
  (31 shorter events, 0.4 us)
Async XLA Ops:
  7.2 76.2 %copy-start = (s32[256]{0:T(256)S(1)}, s32[256]{0:T(256)}, u32[]{:S(2)}) copy-start(s32[256]{0:T(256)} %param.5) | copy-start | bytes 3076
  7.2 131.9 %all-gather.2.cloned.1.call-start = ((), (), s32[]{:S(2)}) async-start(), calls=%async_computation | async-start | bytes 2621440 | tf_op jit(solution)/shard_map/all_gather | solution.py:66
  7.2 43.6 %collective-permute-start = (s32[256]{0:T(256)}, s32[256]{0:T(256)S(1)}, u32[]{:S(2)}, u32[]{:S(2)}) collective-permute-start(s32[256]{0:T(256)} %param.5), channel_id=1, source_target_pairs={{0,1},{1,2},{2,3},{3,4},{4,5},{5,6},{6,7},{7,0},{8,9},{9,10},{10,1... | collective-permute-start | bytes 3080 | tf_op jit(solution)/shard_map/ppermute | solution.py:52
  50.8 4.8 %collective-permute-start.1 = (s32[256]{0:T(256)S(1)}, s32[256]{0:T(256)S(1)}, u32[]{:S(2)}, u32[]{:S(2)}) collective-permute-start(s32[256]{0:T(256)S(1)} %collective-permute-done), channel_id=1, source_target_pairs={{0,1},{1,2},{2,3},{3,4},{4,5},{5,6},{6,7},{7,0},{8,9},{9,10},{10,1... | collective-permute-start | bytes 3080 | tf_op jit(solution)/shard_map/ppermute | solution.py:52
  55.7 5.2 %collective-permute-start.2 = (s32[256]{0:T(256)S(1)}, s32[256]{0:T(256)S(1)}, u32[]{:S(2)}, u32[]{:S(2)}) collective-permute-start(s32[256]{0:T(256)S(1)} %collective-permute-done.1), channel_id=1, source_target_pairs={{0,1},{1,2},{2,3},{3,4},{4,5},{5,6},{6,7},{7,0},{8,9},{9,10},{10,1... | collective-permute-start | bytes 3080 | tf_op jit(solution)/shard_map/ppermute | solution.py:52
  60.9 4.8 %collective-permute-start.3 = (s32[256]{0:T(256)S(1)}, s32[256]{0:T(256)S(1)}, u32[]{:S(2)}, u32[]{:S(2)}) collective-permute-start(s32[256]{0:T(256)S(1)} %collective-permute-done.2), channel_id=1, source_target_pairs={{0,1},{1,2},{2,3},{3,4},{4,5},{5,6},{6,7},{7,0},{8,9},{9,10},{10,1... | collective-permute-start | bytes 3080 | tf_op jit(solution)/shard_map/ppermute | solution.py:52
  65.8 4.8 %collective-permute-start.4 = (s32[256]{0:T(256)S(1)}, s32[256]{0:T(256)S(1)}, u32[]{:S(2)}, u32[]{:S(2)}) collective-permute-start(s32[256]{0:T(256)S(1)} %collective-permute-done.3), channel_id=1, source_target_pairs={{0,1},{1,2},{2,3},{3,4},{4,5},{5,6},{6,7},{7,0},{8,9},{9,10},{10,1... | collective-permute-start | bytes 3080 | tf_op jit(solution)/shard_map/ppermute | solution.py:52
  70.6 4.8 %collective-permute-start.5 = (s32[256]{0:T(256)S(1)}, s32[256]{0:T(256)S(1)}, u32[]{:S(2)}, u32[]{:S(2)}) collective-permute-start(s32[256]{0:T(256)S(1)} %collective-permute-done.4), channel_id=1, source_target_pairs={{0,1},{1,2},{2,3},{3,4},{4,5},{5,6},{6,7},{7,0},{8,9},{9,10},{10,1... | collective-permute-start | bytes 3080 | tf_op jit(solution)/shard_map/ppermute | solution.py:52
  75.4 7.9 %collective-permute-start.6 = (s32[256]{0:T(256)S(1)}, s32[256]{0:T(256)S(1)}, u32[]{:S(2)}, u32[]{:S(2)}) collective-permute-start(s32[256]{0:T(256)S(1)} %collective-permute-done.5), channel_id=1, source_target_pairs={{0,1},{1,2},{2,3},{3,4},{4,5},{5,6},{6,7},{7,0},{8,9},{9,10},{10,1... | collective-permute-start | bytes 3080 | tf_op jit(solution)/shard_map/ppermute | solution.py:52
  110.8 3.4 %slice-start = ((s8[8388608]{0:T(1024)(128)(4,1)}), s8[4194304]{0:T(1024)(128)(4,1)S(1)}, s32[]{:S(2)}) async-start(s8[8388608]{0:T(1024)(128)(4,1)} %bitcast.65), calls=%async_computation.1 | async-start | bytes 8388608
  111.7 3.1 %slice-start.1 = ((s8[8388608]{0:T(1024)(128)(4,1)}), s8[4194304]{0:T(1024)(128)(4,1)S(1)}, s32[]{:S(2)}) async-start(s8[8388608]{0:T(1024)(128)(4,1)} %bitcast.65), calls=%async_computation.2 | async-start | bytes 8388608
Sparse Core Ops, SparseCore 0:
  104.5 34.5 all-gather.1
